TPU v7x, 32 devices: a whole 2x2x4 slice. The times are simulated.
32 devices in a mesh: image: 4 (over y, x), space: 8 (over z, core).
Axes of the slice: x: 2, y: 2, z: 4, core: 2. Of those that a mesh axis runs over, the one named last changes fastest.
Arguments:
- displacement: float32 [4, 3, 8192], P('image', None, 'space'), may hold values from -0.5 to 0.5
- end_states: float32 [2, 3, 8192], P(None, None, 'space'), may hold values from -0.5 to 0.5
- atom_live: int32 [8192], P('space'), may hold values 0 or 1
- partner_cells: int32 [64, 5], P('space'), may hold values from 0 to 11, as said below
- partner_live: int32 [64, 5], P('space'), may hold values from 0 to 1
- spring_const: float32 [4], P('image'), may hold values from 2 to 20
Outputs:
- band_force: float32 [4, 3, 8192], P('image', None, 'space')
- path_stats: float32 [4, 3], P('image')
Inputs may be any that keep to these rules, and one draw needn't show every extreme that they name: `partner_cells`: each cell's live entries name the cell itself (index c + 2), the cells c + 1 and c + 3, and for some cells c or c + 4; the live entries are symmetric between cells of the image (counting cells modulo 64); entries come in any order and dead entries name arbitrary cells.
All inputs are finite; a program needn't handle non-finite values. No bound on the sum of `atom_live` on one device may be relied on, other than what follows from the above.
Results may differ from a plain program's by a relative error of at most 0.0003.
Values sent between devices are 32-bit elements; how exact they have to be, the bound alone decides.
A program may use at most 64 MiB of HBM per device.

v0:
```python
import jax
import jax.numpy as jnp
from jax import lax
from jax.sharding import PartitionSpec as P

SLOTS = 128
GHOST = 2
ITERATIONS = 6


cutoff_sq = 9.0
pair_strength = 0.4
step_size = 0.02
epsilon = 1e-06
tile_block = 2


def shifted(block, axis, distance):
    devices = range(lax.axis_size(axis))
    route = [(i - distance, i) for i in devices if i - distance in devices]
    return lax.ppermute(block, axis, route)


def extended_2(cells, sides, width):
    for axis, dim in sides:
        count = lax.axis_size(axis)
        head = lax.slice_in_dim(cells, 0, width, axis=dim)
        tail = lax.slice_in_dim(cells, cells.shape[dim] - width, cells.shape[dim], axis=dim)
        cells = jnp.concatenate(
            [
                lax.ppermute(tail, axis, [(i, (i + 1) % count) for i in range(count)]),
                cells,
                lax.ppermute(head, axis, [((i + 1) % count, i) for i in range(count)]),
            ],
            axis=dim,
        )
    return cells


def site_table():
    slot_ids = jnp.arange(SLOTS, dtype=jnp.int32)
    return jnp.stack([slot_ids // 64, slot_ids // 8 % 8, slot_ids % 8]).astype(jnp.float32)


def tile_weight(own_live, partner_atoms, tile_live, self_tile, partner):
    diagonal = (
        jnp.arange(SLOTS, dtype=jnp.int32)[:, None] == jnp.arange(SLOTS, dtype=jnp.int32)[None, :]
    )
    weight = (
        own_live[:, :, None]
        * partner_atoms[:, partner, None, :]
        * tile_live[:, partner, None, None]
    )
    return jnp.where(self_tile[:, partner, None, None] & diagonal[None], jnp.float32(0.0), weight)


def pair_geometry(own_sites, partner_sites, partner):
    separation = own_sites[:, :, :, None] - partner_sites[:, partner, :, None, :]
    scaled = jnp.sum(separation * separation, axis=1) / cutoff_sq
    remain = jnp.where(scaled < 1.0, 1.0 - scaled, jnp.float32(0.0))
    return (separation, remain)


def density_cells(own_sites, partner_sites, own_live, partner_atoms, tile_live, self_tile):
    density = jnp.zeros(own_live.shape, jnp.float32)
    for partner in range(partner_sites.shape[1]):
        separation, remain = pair_geometry(own_sites, partner_sites, partner)
        weight = tile_weight(own_live, partner_atoms, tile_live, self_tile, partner)
        density = density + jnp.sum(weight * remain**4, axis=-1)
    return density


def force_cells(
    own_sites,
    partner_sites,
    own_live,
    partner_atoms,
    tile_live,
    self_tile,
    own_slope,
    partner_slope,
):
    total = jnp.zeros(own_sites.shape, jnp.float32)
    for partner in range(partner_sites.shape[1]):
        separation, remain = pair_geometry(own_sites, partner_sites, partner)
        weight = tile_weight(own_live, partner_atoms, tile_live, self_tile, partner)
        slopes = own_slope[:, :, None] + partner_slope[:, partner, None, :]
        coefficient = slopes * (-4.0 * remain**3) + pair_strength * (-3.0 * remain**2)
        total = total + jnp.sum((weight * coefficient)[:, None] * separation, axis=-1)
    return -(2.0 / cutoff_sq) * total


def blocked(function, block_cells, *arrays):
    total_rows = arrays[0].shape[0]
    shaped = tuple(
        (item.reshape((total_rows // block_cells, block_cells) + item.shape[1:]) for item in arrays)
    )
    result = lax.map(lambda group: function(*group), shaped)
    return result.reshape((total_rows,) + result.shape[2:])


def body(displacement, end_states, atom_live, partner_cells, partner_live, spring_const):
    cell_count = partner_cells.shape[0]
    extended_cells = cell_count + 2 * GHOST
    live_flat = atom_live.astype(jnp.float32)
    own_live = live_flat.reshape(cell_count, SLOTS)
    tile_live = partner_live.astype(jnp.float32)
    self_tile = partner_cells == (GHOST + jnp.arange(cell_count, dtype=jnp.int32))[:, None]
    site = site_table()
    axis_unit = jnp.array([1.0, 0.0, 0.0], jnp.float32)
    cell_offsets = (2 * jnp.arange(extended_cells, dtype=jnp.int32)).astype(jnp.float32)
    image_index = lax.axis_index("image")
    image_count = lax.axis_size("image")
    moved = displacement
    for iteration in range(ITERATIONS):
        upstream = shifted(moved, "image", 1)
        downstream = shifted(moved, "image", -1)
        upstream = jnp.where(image_index == 0, end_states[0:1], upstream)
        downstream = jnp.where(image_index == image_count - 1, end_states[1:2], downstream)
        forward_gap = (downstream - moved)[0] * live_flat
        backward_gap = (moved - upstream)[0] * live_flat
        forward_sq, backward_sq, cross_sum = lax.psum(
            (
                jnp.sum(forward_gap * forward_gap),
                jnp.sum(backward_gap * backward_gap),
                jnp.sum(forward_gap * backward_gap),
            ),
            "space",
        )
        packed = jnp.concatenate([moved[0], live_flat[None]], axis=0)
        extended = extended_2(packed, (("space", 1),), GHOST * SLOTS)
        extended = extended.reshape(4, extended_cells, SLOTS)
        placed = (
            extended[:3] + site[:, None, :] + cell_offsets[None, :, None] * axis_unit[:, None, None]
        )
        own_sites = placed[:, GHOST : GHOST + cell_count].transpose(1, 0, 2)
        partner_sites = placed[:, partner_cells].transpose(1, 2, 0, 3)
        partner_atoms = extended[3][partner_cells]
        density = blocked(
            density_cells,
            tile_block,
            own_sites,
            partner_sites,
            own_live,
            partner_atoms,
            tile_live,
            self_tile,
        )
        slope = -0.5 / jnp.sqrt(1.0 + density) * own_live
        slope_wide = extended_2(slope.reshape(-1), (("space", 0),), GHOST * SLOTS)
        slope_all = slope_wide.reshape(extended_cells, SLOTS)
        partner_slope = slope_all[partner_cells]
        force = blocked(
            force_cells,
            tile_block,
            own_sites,
            partner_sites,
            own_live,
            partner_atoms,
            tile_live,
            self_tile,
            slope,
            partner_slope,
        )
        force = force.transpose(1, 0, 2).reshape(3, -1)
        force_ahead, force_behind = lax.psum(
            (jnp.sum(force * forward_gap), jnp.sum(force * backward_gap)), "space"
        )
        length_ahead = jnp.sqrt(forward_sq + epsilon)
        length_behind = jnp.sqrt(backward_sq + epsilon)
        tangent_sq = (
            forward_sq / length_ahead**2
            + backward_sq / length_behind**2
            + 2.0 * cross_sum / (length_ahead * length_behind)
        )
        tangent_len = jnp.sqrt(jnp.maximum(tangent_sq, 1.0))
        tangent = (forward_gap / length_ahead + backward_gap / length_behind) / tangent_len
        parallel = (force_ahead / length_ahead + force_behind / length_behind) / tangent_len
        cosine = cross_sum / (length_ahead * length_behind)
        spring_term = spring_const[0] * (length_ahead - length_behind)
        band_force = force + (spring_term - parallel) * tangent
        path_stats = jnp.stack([parallel, spring_term, cosine])
        moved = moved + step_size * band_force[None]
    return (band_force[None], path_stats[None])


def solution(mesh):
    return jax.shard_map(
        body,
        mesh=mesh,
        in_specs=(
            P("image", None, "space"),
            P(None, None, "space"),
            P("space"),
            P("space", None),
            P("space", None),
            P("image"),
        ),
        out_specs=(P("image", None, "space"), P("image", None)),
        check_vma=False,
    )
```

profile of v0, /device:TPU:0, one launch (start us, length us, event | category | flops | bytes accessed | tf_op | source)
XLA Modules:
  0.0 330.2 jit_solution(6005185140928483629)
XLA Ops:
  0.6 0.7 copy.249
  1.4 1.3 collective-permute-start.4
  2.6 5.5 %collective-permute-start.5 = (f32[1,3,1024]{2,1,0:T(4,128)S(1)}, f32[1,3,1024]{2,1,0:T(4,128)S(1)}, u32[]{:S(2)}, u32[]{:S(2)}) collective-permute-start(f32[1,3,1024]{2,1,0:T(4,128)S(1)} %copy.249), channel_id=1, source_target_pairs={{0,8},{8,16},{16,24},{1,9},{9,17},{17,25},{2,10},{10,18},{18,26},{... | collective-permute-start | bytes 36872 | tf_op jit(solution)/shard_map/ppermute | solution.py:21
  8.2 3.1 collective-permute-start.1
  14.2 1.9 collective-permute-done
  18.1 0.7 slice-done.1
  18.8 6.0 %while.138 = (s32[]{:T(128)}, f32[4,2,128]{2,1,0:T(2,128)S(1)}, pred[4,2,5]{2,1,0:T(4,128)(4,1)S(1)}, f32[4,2,128]{2,1,0:T(2,128)S(1)}, f32[4,2,5,128]{3,1,2,0:T...) while((s32[]{:T(128)}, f32[4,2,128]{2,1,0:T(2,128)S(1)}, ...), condition=%wide.region_11.12_spmd, body=%wide.region_0.11_spmd.sunk | while | flops 3292930 | bytes 1487227 | solution.py:98
  24.8 1.1 collective-permute-start.3
  25.9 1.3 collective-permute-done.3
  27.2 3.5 %collective-permute-done.2 = f32[256]{0:T(256)S(1)} collective-permute-done((f32[256]{0:T(256)S(1)}, f32[256]{0:T(256)S(1)}, u32[]{:S(2)}, u32[]{:S(2)}) %collective-permute-start.2) | collective-permute-done | bytes 1056 | tf_op jit(solution)/shard_map/ppermute | solution.py:31
  31.3 9.4 %while.139 = (s32[]{:T(128)}, f32[4,2,3,128]{3,1,0,2:T(2,128)S(1)}, pred[4,2,5]{2,1,0:T(4,128)(4,1)S(1)}, f32[4,2,128]{2,1,0:T(2,128)S(1)}, f32[4,2,5,128]{3,1,2...) while((s32[]{:T(128)}, f32[4,2,3,128]{3,1,0,2:T(2,128)S(1)}, ...), condition=%wide.region_23.24_spmd, body=%wide.region_12.23_spmd.sunk | while | flops 5423106 | bytes 2878859 | solution.py:98
  41.4 0.7 multiply_reduce_fusion.75
  42.1 0.7 fusion.279
  42.8 14.3 %all-reduce.5 = (f32[]{:T(128)}, f32[]{:T(128)}, f32[]{:T(128)}, f32[]{:T(128)}, f32[]{:T(128)}) all-reduce(f32[]{:T(128)} %get-tuple-element.1555, f32[]{:T(128)} %get-tuple-element.1554, f32[]{:T(128)} %get-tuple-element.1553, f32[]{:T(128)} %get-tuple-element.1567, ...), channel_id=1, replica_groups=mesh['image'=4,'space'=8] {'space'}, use_global_device_ids=true, to_apply=%region_25.26 | all-reduce | flops 5 | bytes 40 | tf_op jit(solution)/shard_map/psum | solution.py:122
  62.2 1.3 collective-permute-start.10
  63.5 4.9 %collective-permute-start.11 = (f32[1,3,1024]{2,1,0:T(4,128)S(1)}, f32[1,3,1024]{2,1,0:T(4,128)S(1)}, u32[]{:S(2)}, u32[]{:S(2)}) collective-permute-start(f32[1,3,1024]{2,1,0:T(4,128)S(1)} %multiply_add_fusion.5), channel_id=1, source_target_pairs={{0,8},{8,16},{16,24},{1,9},{9,17},{17,25},{2,10},{10,18},{18,26},{... | collective-permute-start | bytes 36872 | tf_op jit(solution)/shard_map/ppermute | solution.py:21
  70.5 0.7 slice-done.2
  71.1 6.0 %while.140 = (s32[]{:T(128)}, f32[4,2,128]{2,1,0:T(2,128)S(1)}, pred[4,2,5]{2,1,0:T(4,128)(4,1)S(1)}, f32[4,2,128]{2,1,0:T(2,128)S(1)}, f32[4,2,5,128]{3,1,2,0:T...) while((s32[]{:T(128)}, f32[4,2,128]{2,1,0:T(2,128)S(1)}, ...), condition=%wide.region_45.46_spmd, body=%wide.region_34.45_spmd.sunk | while | flops 3292930 | bytes 1487227 | solution.py:98
  77.1 2.9 collective-permute-start.9
  80.0 1.3 collective-permute-done.9
  81.3 3.5 %collective-permute-done.8 = f32[256]{0:T(256)S(1)} collective-permute-done((f32[256]{0:T(256)S(1)}, f32[256]{0:T(256)S(1)}, u32[]{:S(2)}, u32[]{:S(2)}) %collective-permute-start.8) | collective-permute-done | bytes 1056 | tf_op jit(solution)/shard_map/ppermute | solution.py:31
  85.4 9.4 %while.141 = (s32[]{:T(128)}, f32[4,2,3,128]{3,1,0,2:T(2,128)S(1)}, pred[4,2,5]{2,1,0:T(4,128)(4,1)S(1)}, f32[4,2,128]{2,1,0:T(2,128)S(1)}, f32[4,2,5,128]{3,1,2...) while((s32[]{:T(128)}, f32[4,2,3,128]{3,1,0,2:T(2,128)S(1)}, ...), condition=%wide.region_57.58_spmd, body=%wide.region_46.57_spmd.sunk | while | flops 5423106 | bytes 2878859 | solution.py:98
  94.9 0.7 multiply_reduce_fusion.72
  96.3 14.3 %all-reduce.4 = (f32[]{:T(128)}, f32[]{:T(128)}, f32[]{:T(128)}, f32[]{:T(128)}, f32[]{:T(128)}) all-reduce(f32[]{:T(128)} %get-tuple-element.1552, f32[]{:T(128)} %get-tuple-element.1551, f32[]{:T(128)} %get-tuple-element.1550, f32[]{:T(128)} %get-tuple-element.1565, ...), channel_id=1, replica_groups=mesh['image'=4,'space'=8] {'space'}, use_global_device_ids=true, to_apply=%region_59.60 | all-reduce | flops 5 | bytes 40 | tf_op jit(solution)/shard_map/psum | solution.py:122
  115.7 1.3 collective-permute-start.16
  117.0 5.2 %collective-permute-start.17 = (f32[1,3,1024]{2,1,0:T(4,128)S(1)}, f32[1,3,1024]{2,1,0:T(4,128)S(1)}, u32[]{:S(2)}, u32[]{:S(2)}) collective-permute-start(f32[1,3,1024]{2,1,0:T(4,128)S(1)} %multiply_add_fusion.4), channel_id=1, source_target_pairs={{0,8},{8,16},{16,24},{1,9},{9,17},{17,25},{2,10},{10,18},{18,26},{... | collective-permute-start | bytes 36872 | tf_op jit(solution)/shard_map/ppermute | solution.py:21
  123.6 0.7 slice-done.3
  124.3 6.0 %while.142 = (s32[]{:T(128)}, f32[4,2,128]{2,1,0:T(2,128)S(1)}, pred[4,2,5]{2,1,0:T(4,128)(4,1)S(1)}, f32[4,2,128]{2,1,0:T(2,128)S(1)}, f32[4,2,5,128]{3,1,2,0:T...) while((s32[]{:T(128)}, f32[4,2,128]{2,1,0:T(2,128)S(1)}, ...), condition=%wide.region_79.80_spmd, body=%wide.region_68.79_spmd.sunk | while | flops 3292930 | bytes 1487227 | solution.py:98
  130.3 2.9 collective-permute-start.15
  133.2 1.3 collective-permute-done.15
  134.4 3.5 %collective-permute-done.14 = f32[256]{0:T(256)S(1)} collective-permute-done((f32[256]{0:T(256)S(1)}, f32[256]{0:T(256)S(1)}, u32[]{:S(2)}, u32[]{:S(2)}) %collective-permute-start.14) | collective-permute-done | bytes 1056 | tf_op jit(solution)/shard_map/ppermute | solution.py:31
  138.6 9.4 %while.143 = (s32[]{:T(128)}, f32[4,2,3,128]{3,1,0,2:T(2,128)S(1)}, pred[4,2,5]{2,1,0:T(4,128)(4,1)S(1)}, f32[4,2,128]{2,1,0:T(2,128)S(1)}, f32[4,2,5,128]{3,1,2...) while((s32[]{:T(128)}, f32[4,2,3,128]{3,1,0,2:T(2,128)S(1)}, ...), condition=%wide.region_91.92_spmd, body=%wide.region_80.91_spmd.sunk | while | flops 5423106 | bytes 2878859 | solution.py:98
  148.0 0.7 multiply_reduce_fusion.69
  149.4 14.3 %all-reduce.3 = (f32[]{:T(128)}, f32[]{:T(128)}, f32[]{:T(128)}, f32[]{:T(128)}, f32[]{:T(128)}) all-reduce(f32[]{:T(128)} %get-tuple-element.1549, f32[]{:T(128)} %get-tuple-element.1548, f32[]{:T(128)} %get-tuple-element.1547, f32[]{:T(128)} %get-tuple-element.1563, ...), channel_id=1, replica_groups=mesh['image'=4,'space'=8] {'space'}, use_global_device_ids=true, to_apply=%region_93.94 | all-reduce | flops 5 | bytes 40 | tf_op jit(solution)/shard_map/psum | solution.py:122
  168.8 1.3 collective-permute-start.22
  170.1 5.3 %collective-permute-start.23 = (f32[1,3,1024]{2,1,0:T(4,128)S(1)}, f32[1,3,1024]{2,1,0:T(4,128)S(1)}, u32[]{:S(2)}, u32[]{:S(2)}) collective-permute-start(f32[1,3,1024]{2,1,0:T(4,128)S(1)} %multiply_add_fusion.3), channel_id=1, source_target_pairs={{0,8},{8,16},{16,24},{1,9},{9,17},{17,25},{2,10},{10,18},{18,26},{... | collective-permute-start | bytes 36872 | tf_op jit(solution)/shard_map/ppermute | solution.py:21
  176.9 0.7 slice-done.4
  177.6 6.0 %while.144 = (s32[]{:T(128)}, f32[4,2,128]{2,1,0:T(2,128)S(1)}, pred[4,2,5]{2,1,0:T(4,128)(4,1)S(1)}, f32[4,2,128]{2,1,0:T(2,128)S(1)}, f32[4,2,5,128]{3,1,2,0:T...) while((s32[]{:T(128)}, f32[4,2,128]{2,1,0:T(2,128)S(1)}, ...), condition=%wide.region_113.114_spmd, body=%wide.region_102.113_spmd.sunk | while | flops 3292930 | bytes 1487227 | solution.py:98
  183.6 2.9 collective-permute-start.21
  186.5 1.3 collective-permute-done.21
  187.7 3.5 %collective-permute-done.20 = f32[256]{0:T(256)S(1)} collective-permute-done((f32[256]{0:T(256)S(1)}, f32[256]{0:T(256)S(1)}, u32[]{:S(2)}, u32[]{:S(2)}) %collective-permute-start.20) | collective-permute-done | bytes 1056 | tf_op jit(solution)/shard_map/ppermute | solution.py:31
  191.9 9.4 %while.145 = (s32[]{:T(128)}, f32[4,2,3,128]{3,1,0,2:T(2,128)S(1)}, pred[4,2,5]{2,1,0:T(4,128)(4,1)S(1)}, f32[4,2,128]{2,1,0:T(2,128)S(1)}, f32[4,2,5,128]{3,1,2...) while((s32[]{:T(128)}, f32[4,2,3,128]{3,1,0,2:T(2,128)S(1)}, ...), condition=%wide.region_125.126_spmd, body=%wide.region_114.125_spmd.sunk | while | flops 5423106 | bytes 2878859 | solution.py:98
  201.3 0.7 multiply_reduce_fusion.66
  202.7 14.3 %all-reduce.2 = (f32[]{:T(128)}, f32[]{:T(128)}, f32[]{:T(128)}, f32[]{:T(128)}, f32[]{:T(128)}) all-reduce(f32[]{:T(128)} %get-tuple-element.1546, f32[]{:T(128)} %get-tuple-element.1545, f32[]{:T(128)} %get-tuple-element.1544, f32[]{:T(128)} %get-tuple-element.1561, ...), channel_id=1, replica_groups=mesh['image'=4,'space'=8] {'space'}, use_global_device_ids=true, to_apply=%region_127.128 | all-reduce | flops 5 | bytes 40 | tf_op jit(solution)/shard_map/psum | solution.py:122
  222.1 1.3 collective-permute-start.28
  223.4 5.2 %collective-permute-start.29 = (f32[1,3,1024]{2,1,0:T(4,128)S(1)}, f32[1,3,1024]{2,1,0:T(4,128)S(1)}, u32[]{:S(2)}, u32[]{:S(2)}) collective-permute-start(f32[1,3,1024]{2,1,0:T(4,128)S(1)} %multiply_add_fusion.2), channel_id=1, source_target_pairs={{0,8},{8,16},{16,24},{1,9},{9,17},{17,25},{2,10},{10,18},{18,26},{... | collective-permute-start | bytes 36872 | tf_op jit(solution)/shard_map/ppermute | solution.py:21
  230.0 0.7 slice-done.5
  230.7 6.0 %while.146 = (s32[]{:T(128)}, f32[4,2,128]{2,1,0:T(2,128)S(1)}, pred[4,2,5]{2,1,0:T(4,128)(4,1)S(1)}, f32[4,2,128]{2,1,0:T(2,128)S(1)}, f32[4,2,5,128]{3,1,2,0:T...) while((s32[]{:T(128)}, f32[4,2,128]{2,1,0:T(2,128)S(1)}, ...), condition=%wide.region_147.148_spmd, body=%wide.region_136.147_spmd.sunk | while | flops 3292930 | bytes 1487227 | solution.py:98
  236.7 2.9 collective-permute-start.27
  239.6 1.3 collective-permute-done.27
  240.9 3.5 %collective-permute-done.26 = f32[256]{0:T(256)S(1)} collective-permute-done((f32[256]{0:T(256)S(1)}, f32[256]{0:T(256)S(1)}, u32[]{:S(2)}, u32[]{:S(2)}) %collective-permute-start.26) | collective-permute-done | bytes 1056 | tf_op jit(solution)/shard_map/ppermute | solution.py:31
  245.0 9.4 %while.147 = (s32[]{:T(128)}, f32[4,2,3,128]{3,1,0,2:T(2,128)S(1)}, pred[4,2,5]{2,1,0:T(4,128)(4,1)S(1)}, f32[4,2,128]{2,1,0:T(2,128)S(1)}, f32[4,2,5,128]{3,1,2...) while((s32[]{:T(128)}, f32[4,2,3,128]{3,1,0,2:T(2,128)S(1)}, ...), condition=%wide.region_159.160_spmd, body=%wide.region_148.159_spmd.sunk | while | flops 5423106 | bytes 2878859 | solution.py:98
  254.5 0.7 multiply_reduce_fusion.63
  255.8 14.3 %all-reduce.1 = (f32[]{:T(128)}, f32[]{:T(128)}, f32[]{:T(128)}, f32[]{:T(128)}, f32[]{:T(128)}) all-reduce(f32[]{:T(128)} %get-tuple-element.1543, f32[]{:T(128)} %get-tuple-element.1542, f32[]{:T(128)} %get-tuple-element.1541, f32[]{:T(128)} %get-tuple-element.1559, ...), channel_id=1, replica_groups=mesh['image'=4,'space'=8] {'space'}, use_global_device_ids=true, to_apply=%region_161.162 | all-reduce | flops 5 | bytes 40 | tf_op jit(solution)/shard_map/psum | solution.py:122
  275.2 1.3 collective-permute-start.34
  276.5 5.2 %collective-permute-start.35 = (f32[1,3,1024]{2,1,0:T(4,128)S(1)}, f32[1,3,1024]{2,1,0:T(4,128)S(1)}, u32[]{:S(2)}, u32[]{:S(2)}) collective-permute-start(f32[1,3,1024]{2,1,0:T(4,128)S(1)} %multiply_add_fusion.1), channel_id=1, source_target_pairs={{0,8},{8,16},{16,24},{1,9},{9,17},{17,25},{2,10},{10,18},{18,26},{... | collective-permute-start | bytes 36872 | tf_op jit(solution)/shard_map/ppermute | solution.py:21
  283.7 0.7 slice-done
  284.4 6.0 %while.148 = (s32[]{:T(128)}, f32[4,2,128]{2,1,0:T(2,128)S(1)}, pred[4,2,5]{2,1,0:T(4,128)(4,1)S(1)}, f32[4,2,128]{2,1,0:T(2,128)S(1)}, f32[4,2,5,128]{3,1,2,0:T...) while((s32[]{:T(128)}, f32[4,2,128]{2,1,0:T(2,128)S(1)}, ...), condition=%wide.region_181.182_spmd, body=%wide.region_170.181_spmd.sunk | while | flops 3292930 | bytes 1487227 | solution.py:98
  290.4 2.9 collective-permute-start.33
  293.3 1.3 collective-permute-done.33
  294.6 3.5 %collective-permute-done.32 = f32[256]{0:T(256)S(1)} collective-permute-done((f32[256]{0:T(256)S(1)}, f32[256]{0:T(256)S(1)}, u32[]{:S(2)}, u32[]{:S(2)}) %collective-permute-start.32) | collective-permute-done | bytes 1056 | tf_op jit(solution)/shard_map/ppermute | solution.py:31
  298.7 9.4 %while.149 = (s32[]{:T(128)}, f32[4,2,3,128]{3,1,0,2:T(2,128)S(1)}, pred[4,2,5]{2,1,0:T(4,128)(4,1)S(1)}, f32[4,2,128]{2,1,0:T(2,128)S(1)}, f32[4,2,5,128]{3,1,2...) while((s32[]{:T(128)}, f32[4,2,3,128]{3,1,0,2:T(2,128)S(1)}, ...), condition=%wide.region_193.194_spmd, body=%wide.region_182.193_spmd.sunk | while | flops 5423106 | bytes 2878859 | solution.py:98
  308.2 0.7 multiply_reduce_fusion.60
  309.5 14.3 %all-reduce = (f32[]{:T(128)}, f32[]{:T(128)}, f32[]{:T(128)}, f32[]{:T(128)}, f32[]{:T(128)}) all-reduce(f32[]{:T(128)} %get-tuple-element.1540, f32[]{:T(128)} %get-tuple-element.1539, f32[]{:T(128)} %get-tuple-element.1538, f32[]{:T(128)} %get-tuple-element.1557, ...), channel_id=1, replica_groups=mesh['image'=4,'space'=8] {'space'}, use_global_device_ids=true, to_apply=%region_195.196 | all-reduce | flops 5 | bytes 40 | tf_op jit(solution)/shard_map/psum | solution.py:122
  (1033 shorter events, 111.3 us)
Async XLA Ops:
  0.6 7.5 %copy-start.6 = (s32[1024]{0:T(1024)S(1)}, s32[1024]{0:T(1024)}, u32[]{:S(2)}) copy-start(s32[1024]{0:T(1024)} %param.33) | copy-start | bytes 12292
  1.4 39.4 %collective-permute-start.4 = (f32[1,3,1024]{2,1,0:T(4,128)S(1)}, f32[1,3,1024]{2,1,0:T(4,128)S(1)}, u32[]{:S(2)}, u32[]{:S(2)}) collective-permute-start(f32[1,3,1024]{2,1,0:T(4,128)S(1)} %copy.249), channel_id=1, source_target_pairs={{8,0},{16,8},{24,16},{9,1},{17,9},{25,17},{10,2},{18,10},{26,18},{... | collective-permute-start | bytes 36872 | tf_op jit(solution)/shard_map/ppermute | solution.py:21
  2.6 38.1 %collective-permute-start.5 = (f32[1,3,1024]{2,1,0:T(4,128)S(1)}, f32[1,3,1024]{2,1,0:T(4,128)S(1)}, u32[]{:S(2)}, u32[]{:S(2)}) collective-permute-start(f32[1,3,1024]{2,1,0:T(4,128)S(1)} %copy.249), channel_id=1, source_target_pairs={{0,8},{8,16},{16,24},{1,9},{9,17},{17,25},{2,10},{10,18},{18,26},{... | collective-permute-start | bytes 36872 | tf_op jit(solution)/shard_map/ppermute | solution.py:21
  8.2 3.9 %copy-start.8 = (f32[2,3,1024]{2,0,1:T(2,128)S(1)}, f32[2,3,1024]{2,0,1:T(2,128)}, u32[]{:S(2)}) copy-start(f32[2,3,1024]{2,0,1:T(2,128)} %param.32) | copy-start | bytes 73732
  8.2 6.0 %collective-permute-start.1 = (f32[4,256]{1,0:T(4,128)S(1)}, f32[4,256]{1,0:T(4,128)S(1)}, u32[]{:S(2)}, u32[]{:S(2)}) collective-permute-start(f32[4,256]{1,0:T(4,128)S(1)} %get-tuple-element.2043), channel_id=1, source_target_pairs={{1,0},{2,1},{3,2},{4,3},{5,4},{6,5},{7,6},{0,7},{9,8},{10,9},{11,1... | collective-permute-start | bytes 12296 | tf_op jit(solution)/shard_map/ppermute | solution.py:33
  11.3 0.7 copy-start.9
  11.3 4.8 %collective-permute-start = (f32[4,256]{1,0:T(4,128)S(1)}, f32[4,256]{1,0:T(4,128)S(1)}, u32[]{:S(2)}, u32[]{:S(2)}) collective-permute-start(f32[4,256]{1,0:T(4,128)S(1)} %get-tuple-element.2042), channel_id=1, source_target_pairs={{0,1},{1,2},{2,3},{3,4},{4,5},{5,6},{6,7},{7,0},{8,9},{9,10},{10,1... | collective-permute-start | bytes 12296 | tf_op jit(solution)/shard_map/ppermute | solution.py:31
  12.1 0.7 copy-start.11
  12.9 0.7 copy-start.10
  16.2 0.6 copy-start.1
  18.0 0.7 slice-start.1
  24.8 2.4 collective-permute-start.3
  25.9 4.8 %collective-permute-start.2 = (f32[256]{0:T(256)S(1)}, f32[256]{0:T(256)S(1)}, u32[]{:S(2)}, u32[]{:S(2)}) collective-permute-start(f32[256]{0:T(256)S(1)} %get-tuple-element.2068), channel_id=1, source_target_pairs={{0,1},{1,2},{2,3},{3,4},{4,5},{5,6},{6,7},{7,0},{8,9},{9,10},{10,1... | collective-permute-start | bytes 3080 | tf_op jit(solution)/shard_map/ppermute | solution.py:31
  40.7 0.7 copy-start.7
  61.7 6.8 %collective-permute-start.7 = (f32[4,256]{1,0:T(4,128)S(1)}, f32[4,256]{1,0:T(4,128)S(1)}, u32[]{:S(2)}, u32[]{:S(2)}) collective-permute-start(f32[4,256]{1,0:T(4,128)S(1)} %get-tuple-element.2041), channel_id=1, source_target_pairs={{1,0},{2,1},{3,2},{4,3},{5,4},{6,5},{7,6},{0,7},{9,8},{10,9},{11,1... | collective-permute-start | bytes 12296 | tf_op jit(solution)/shard_map/ppermute | solution.py:33
  61.7 6.7 %collective-permute-start.6 = (f32[4,256]{1,0:T(4,128)S(1)}, f32[4,256]{1,0:T(4,128)S(1)}, u32[]{:S(2)}, u32[]{:S(2)}) collective-permute-start(f32[4,256]{1,0:T(4,128)S(1)} %get-tuple-element.2040), channel_id=1, source_target_pairs={{0,1},{1,2},{2,3},{3,4},{4,5},{5,6},{6,7},{7,0},{8,9},{9,10},{10,1... | collective-permute-start | bytes 12296 | tf_op jit(solution)/shard_map/ppermute | solution.py:31
  62.2 32.7 %collective-permute-start.10 = (f32[1,3,1024]{2,1,0:T(4,128)S(1)}, f32[1,3,1024]{2,1,0:T(4,128)S(1)}, u32[]{:S(2)}, u32[]{:S(2)}) collective-permute-start(f32[1,3,1024]{2,1,0:T(4,128)S(1)} %multiply_add_fusion.5), channel_id=1, source_target_pairs={{8,0},{16,8},{24,16},{9,1},{17,9},{25,17},{10,2},{18,10},{26,18},{... | collective-permute-start | bytes 36872 | tf_op jit(solution)/shard_map/ppermute | solution.py:21
  63.5 31.4 %collective-permute-start.11 = (f32[1,3,1024]{2,1,0:T(4,128)S(1)}, f32[1,3,1024]{2,1,0:T(4,128)S(1)}, u32[]{:S(2)}, u32[]{:S(2)}) collective-permute-start(f32[1,3,1024]{2,1,0:T(4,128)S(1)} %multiply_add_fusion.5), channel_id=1, source_target_pairs={{0,8},{8,16},{16,24},{1,9},{9,17},{17,25},{2,10},{10,18},{18,26},{... | collective-permute-start | bytes 36872 | tf_op jit(solution)/shard_map/ppermute | solution.py:21
  68.6 0.6 copy-start.2
  70.4 0.7 slice-start.2
  77.1 4.2 %collective-permute-start.9 = (f32[256]{0:T(256)S(1)}, f32[256]{0:T(256)S(1)}, u32[]{:S(2)}, u32[]{:S(2)}) collective-permute-start(f32[256]{0:T(256)S(1)} %get-tuple-element.2063), channel_id=1, source_target_pairs={{1,0},{2,1},{3,2},{4,3},{5,4},{6,5},{7,6},{0,7},{9,8},{10,9},{11,1... | collective-permute-start | bytes 3080 | tf_op jit(solution)/shard_map/ppermute | solution.py:33
  80.0 4.8 %collective-permute-start.8 = (f32[256]{0:T(256)S(1)}, f32[256]{0:T(256)S(1)}, u32[]{:S(2)}, u32[]{:S(2)}) collective-permute-start(f32[256]{0:T(256)S(1)} %get-tuple-element.2062), channel_id=1, source_target_pairs={{0,1},{1,2},{2,3},{3,4},{4,5},{5,6},{6,7},{7,0},{8,9},{9,10},{10,1... | collective-permute-start | bytes 3080 | tf_op jit(solution)/shard_map/ppermute | solution.py:31
  115.1 7.0 %collective-permute-start.13 = (f32[4,256]{1,0:T(4,128)S(1)}, f32[4,256]{1,0:T(4,128)S(1)}, u32[]{:S(2)}, u32[]{:S(2)}) collective-permute-start(f32[4,256]{1,0:T(4,128)S(1)} %get-tuple-element.2039), channel_id=1, source_target_pairs={{1,0},{2,1},{3,2},{4,3},{5,4},{6,5},{7,6},{0,7},{9,8},{10,9},{11,1... | collective-permute-start | bytes 12296 | tf_op jit(solution)/shard_map/ppermute | solution.py:33
  115.2 7.0 %collective-permute-start.12 = (f32[4,256]{1,0:T(4,128)S(1)}, f32[4,256]{1,0:T(4,128)S(1)}, u32[]{:S(2)}, u32[]{:S(2)}) collective-permute-start(f32[4,256]{1,0:T(4,128)S(1)} %get-tuple-element.2038), channel_id=1, source_target_pairs={{0,1},{1,2},{2,3},{3,4},{4,5},{5,6},{6,7},{7,0},{8,9},{9,10},{10,1... | collective-permute-start | bytes 12296 | tf_op jit(solution)/shard_map/ppermute | solution.py:31
  115.7 32.3 %collective-permute-start.16 = (f32[1,3,1024]{2,1,0:T(4,128)S(1)}, f32[1,3,1024]{2,1,0:T(4,128)S(1)}, u32[]{:S(2)}, u32[]{:S(2)}) collective-permute-start(f32[1,3,1024]{2,1,0:T(4,128)S(1)} %multiply_add_fusion.4), channel_id=1, source_target_pairs={{8,0},{16,8},{24,16},{9,1},{17,9},{25,17},{10,2},{18,10},{26,18},{... | collective-permute-start | bytes 36872 | tf_op jit(solution)/shard_map/ppermute | solution.py:21
  117.0 31.1 %collective-permute-start.17 = (f32[1,3,1024]{2,1,0:T(4,128)S(1)}, f32[1,3,1024]{2,1,0:T(4,128)S(1)}, u32[]{:S(2)}, u32[]{:S(2)}) collective-permute-start(f32[1,3,1024]{2,1,0:T(4,128)S(1)} %multiply_add_fusion.4), channel_id=1, source_target_pairs={{0,8},{8,16},{16,24},{1,9},{9,17},{17,25},{2,10},{10,18},{18,26},{... | collective-permute-start | bytes 36872 | tf_op jit(solution)/shard_map/ppermute | solution.py:21
  122.3 0.6 copy-start.3
  123.5 0.7 slice-start.3
  130.3 4.2 %collective-permute-start.15 = (f32[256]{0:T(256)S(1)}, f32[256]{0:T(256)S(1)}, u32[]{:S(2)}, u32[]{:S(2)}) collective-permute-start(f32[256]{0:T(256)S(1)} %get-tuple-element.2059), channel_id=1, source_target_pairs={{1,0},{2,1},{3,2},{4,3},{5,4},{6,5},{7,6},{0,7},{9,8},{10,9},{11,1... | collective-permute-start | bytes 3080 | tf_op jit(solution)/shard_map/ppermute | solution.py:33
  133.1 4.8 %collective-permute-start.14 = (f32[256]{0:T(256)S(1)}, f32[256]{0:T(256)S(1)}, u32[]{:S(2)}, u32[]{:S(2)}) collective-permute-start(f32[256]{0:T(256)S(1)} %get-tuple-element.2058), channel_id=1, source_target_pairs={{0,1},{1,2},{2,3},{3,4},{4,5},{5,6},{6,7},{7,0},{8,9},{9,10},{10,1... | collective-permute-start | bytes 3080 | tf_op jit(solution)/shard_map/ppermute | solution.py:31
  168.2 7.2 %collective-permute-start.19 = (f32[4,256]{1,0:T(4,128)S(1)}, f32[4,256]{1,0:T(4,128)S(1)}, u32[]{:S(2)}, u32[]{:S(2)}) collective-permute-start(f32[4,256]{1,0:T(4,128)S(1)} %get-tuple-element.2037), channel_id=1, source_target_pairs={{1,0},{2,1},{3,2},{4,3},{5,4},{6,5},{7,6},{0,7},{9,8},{10,9},{11,1... | collective-permute-start | bytes 12296 | tf_op jit(solution)/shard_map/ppermute | solution.py:33
  168.3 7.2 %collective-permute-start.18 = (f32[4,256]{1,0:T(4,128)S(1)}, f32[4,256]{1,0:T(4,128)S(1)}, u32[]{:S(2)}, u32[]{:S(2)}) collective-permute-start(f32[4,256]{1,0:T(4,128)S(1)} %get-tuple-element.2036), channel_id=1, source_target_pairs={{0,1},{1,2},{2,3},{3,4},{4,5},{5,6},{6,7},{7,0},{8,9},{9,10},{10,1... | collective-permute-start | bytes 12296 | tf_op jit(solution)/shard_map/ppermute | solution.py:31
  168.8 32.5 %collective-permute-start.22 = (f32[1,3,1024]{2,1,0:T(4,128)S(1)}, f32[1,3,1024]{2,1,0:T(4,128)S(1)}, u32[]{:S(2)}, u32[]{:S(2)}) collective-permute-start(f32[1,3,1024]{2,1,0:T(4,128)S(1)} %multiply_add_fusion.3), channel_id=1, source_target_pairs={{8,0},{16,8},{24,16},{9,1},{17,9},{25,17},{10,2},{18,10},{26,18},{... | collective-permute-start | bytes 36872 | tf_op jit(solution)/shard_map/ppermute | solution.py:21
  170.1 31.2 %collective-permute-start.23 = (f32[1,3,1024]{2,1,0:T(4,128)S(1)}, f32[1,3,1024]{2,1,0:T(4,128)S(1)}, u32[]{:S(2)}, u32[]{:S(2)}) collective-permute-start(f32[1,3,1024]{2,1,0:T(4,128)S(1)} %multiply_add_fusion.3), channel_id=1, source_target_pairs={{0,8},{8,16},{16,24},{1,9},{9,17},{17,25},{2,10},{10,18},{18,26},{... | collective-permute-start | bytes 36872 | tf_op jit(solution)/shard_map/ppermute | solution.py:21
  175.6 0.6 copy-start.4
  176.8 0.7 slice-start.4
  183.6 4.2 %collective-permute-start.21 = (f32[256]{0:T(256)S(1)}, f32[256]{0:T(256)S(1)}, u32[]{:S(2)}, u32[]{:S(2)}) collective-permute-start(f32[256]{0:T(256)S(1)} %get-tuple-element.2055), channel_id=1, source_target_pairs={{1,0},{2,1},{3,2},{4,3},{5,4},{6,5},{7,6},{0,7},{9,8},{10,9},{11,1... | collective-permute-start | bytes 3080 | tf_op jit(solution)/shard_map/ppermute | solution.py:33
  186.4 4.8 %collective-permute-start.20 = (f32[256]{0:T(256)S(1)}, f32[256]{0:T(256)S(1)}, u32[]{:S(2)}, u32[]{:S(2)}) collective-permute-start(f32[256]{0:T(256)S(1)} %get-tuple-element.2054), channel_id=1, source_target_pairs={{0,1},{1,2},{2,3},{3,4},{4,5},{5,6},{6,7},{7,0},{8,9},{9,10},{10,1... | collective-permute-start | bytes 3080 | tf_op jit(solution)/shard_map/ppermute | solution.py:31
  221.5 7.0 %collective-permute-start.25 = (f32[4,256]{1,0:T(4,128)S(1)}, f32[4,256]{1,0:T(4,128)S(1)}, u32[]{:S(2)}, u32[]{:S(2)}) collective-permute-start(f32[4,256]{1,0:T(4,128)S(1)} %get-tuple-element.2035), channel_id=1, source_target_pairs={{1,0},{2,1},{3,2},{4,3},{5,4},{6,5},{7,6},{0,7},{9,8},{10,9},{11,1... | collective-permute-start | bytes 12296 | tf_op jit(solution)/shard_map/ppermute | solution.py:33
  221.6 7.0 %collective-permute-start.24 = (f32[4,256]{1,0:T(4,128)S(1)}, f32[4,256]{1,0:T(4,128)S(1)}, u32[]{:S(2)}, u32[]{:S(2)}) collective-permute-start(f32[4,256]{1,0:T(4,128)S(1)} %get-tuple-element.2034), channel_id=1, source_target_pairs={{0,1},{1,2},{2,3},{3,4},{4,5},{5,6},{6,7},{7,0},{8,9},{9,10},{10,1... | collective-permute-start | bytes 12296 | tf_op jit(solution)/shard_map/ppermute | solution.py:31
  222.1 32.3 %collective-permute-start.28 = (f32[1,3,1024]{2,1,0:T(4,128)S(1)}, f32[1,3,1024]{2,1,0:T(4,128)S(1)}, u32[]{:S(2)}, u32[]{:S(2)}) collective-permute-start(f32[1,3,1024]{2,1,0:T(4,128)S(1)} %multiply_add_fusion.2), channel_id=1, source_target_pairs={{8,0},{16,8},{24,16},{9,1},{17,9},{25,17},{10,2},{18,10},{26,18},{... | collective-permute-start | bytes 36872 | tf_op jit(solution)/shard_map/ppermute | solution.py:21
  223.4 31.1 %collective-permute-start.29 = (f32[1,3,1024]{2,1,0:T(4,128)S(1)}, f32[1,3,1024]{2,1,0:T(4,128)S(1)}, u32[]{:S(2)}, u32[]{:S(2)}) collective-permute-start(f32[1,3,1024]{2,1,0:T(4,128)S(1)} %multiply_add_fusion.2), channel_id=1, source_target_pairs={{0,8},{8,16},{16,24},{1,9},{9,17},{17,25},{2,10},{10,18},{18,26},{... | collective-permute-start | bytes 36872 | tf_op jit(solution)/shard_map/ppermute | solution.py:21
  228.7 0.6 copy-start.5
  230.0 0.7 slice-start.5
  236.7 4.2 %collective-permute-start.27 = (f32[256]{0:T(256)S(1)}, f32[256]{0:T(256)S(1)}, u32[]{:S(2)}, u32[]{:S(2)}) collective-permute-start(f32[256]{0:T(256)S(1)} %get-tuple-element.2051), channel_id=1, source_target_pairs={{1,0},{2,1},{3,2},{4,3},{5,4},{6,5},{7,6},{0,7},{9,8},{10,9},{11,1... | collective-permute-start | bytes 3080 | tf_op jit(solution)/shard_map/ppermute | solution.py:33
  239.6 4.8 %collective-permute-start.26 = (f32[256]{0:T(256)S(1)}, f32[256]{0:T(256)S(1)}, u32[]{:S(2)}, u32[]{:S(2)}) collective-permute-start(f32[256]{0:T(256)S(1)} %get-tuple-element.2050), channel_id=1, source_target_pairs={{0,1},{1,2},{2,3},{3,4},{4,5},{5,6},{6,7},{7,0},{8,9},{9,10},{10,1... | collective-permute-start | bytes 3080 | tf_op jit(solution)/shard_map/ppermute | solution.py:31
  274.7 7.0 %collective-permute-start.31 = (f32[4,256]{1,0:T(4,128)S(1)}, f32[4,256]{1,0:T(4,128)S(1)}, u32[]{:S(2)}, u32[]{:S(2)}) collective-permute-start(f32[4,256]{1,0:T(4,128)S(1)} %get-tuple-element.2033), channel_id=1, source_target_pairs={{1,0},{2,1},{3,2},{4,3},{5,4},{6,5},{7,6},{0,7},{9,8},{10,9},{11,1... | collective-permute-start | bytes 12296 | tf_op jit(solution)/shard_map/ppermute | solution.py:33
  274.7 7.0 %collective-permute-start.30 = (f32[4,256]{1,0:T(4,128)S(1)}, f32[4,256]{1,0:T(4,128)S(1)}, u32[]{:S(2)}, u32[]{:S(2)}) collective-permute-start(f32[4,256]{1,0:T(4,128)S(1)} %get-tuple-element.2032), channel_id=1, source_target_pairs={{0,1},{1,2},{2,3},{3,4},{4,5},{5,6},{6,7},{7,0},{8,9},{9,10},{10,1... | collective-permute-start | bytes 12296 | tf_op jit(solution)/shard_map/ppermute | solution.py:31
  275.2 32.9 %collective-permute-start.34 = (f32[1,3,1024]{2,1,0:T(4,128)S(1)}, f32[1,3,1024]{2,1,0:T(4,128)S(1)}, u32[]{:S(2)}, u32[]{:S(2)}) collective-permute-start(f32[1,3,1024]{2,1,0:T(4,128)S(1)} %multiply_add_fusion.1), channel_id=1, source_target_pairs={{8,0},{16,8},{24,16},{9,1},{17,9},{25,17},{10,2},{18,10},{26,18},{... | collective-permute-start | bytes 36872 | tf_op jit(solution)/shard_map/ppermute | solution.py:21
  276.5 31.6 %collective-permute-start.35 = (f32[1,3,1024]{2,1,0:T(4,128)S(1)}, f32[1,3,1024]{2,1,0:T(4,128)S(1)}, u32[]{:S(2)}, u32[]{:S(2)}) collective-permute-start(f32[1,3,1024]{2,1,0:T(4,128)S(1)} %multiply_add_fusion.1), channel_id=1, source_target_pairs={{0,8},{8,16},{16,24},{1,9},{9,17},{17,25},{2,10},{10,18},{18,26},{... | collective-permute-start | bytes 36872 | tf_op jit(solution)/shard_map/ppermute | solution.py:21
  281.8 0.6 copy-start
  283.7 0.7 slice-start
  290.4 4.2 %collective-permute-start.33 = (f32[256]{0:T(256)S(1)}, f32[256]{0:T(256)S(1)}, u32[]{:S(2)}, u32[]{:S(2)}) collective-permute-start(f32[256]{0:T(256)S(1)} %get-tuple-element.2047), channel_id=1, source_target_pairs={{1,0},{2,1},{3,2},{4,3},{5,4},{6,5},{7,6},{0,7},{9,8},{10,9},{11,1... | collective-permute-start | bytes 3080 | tf_op jit(solution)/shard_map/ppermute | solution.py:33
  293.3 4.8 %collective-permute-start.32 = (f32[256]{0:T(256)S(1)}, f32[256]{0:T(256)S(1)}, u32[]{:S(2)}, u32[]{:S(2)}) collective-permute-start(f32[256]{0:T(256)S(1)} %get-tuple-element.2046), channel_id=1, source_target_pairs={{0,1},{1,2},{2,3},{3,4},{4,5},{5,6},{6,7},{7,0},{8,9},{9,10},{10,1... | collective-permute-start | bytes 3080 | tf_op jit(solution)/shard_map/ppermute | solution.py:31
where the time goes:
time: 332 us; the launch traced here: 330 us
  blocking collectives  85.8 us (26%)
  other arithmetic  68.9 us (21%)
  starting transfers between devices  60.3 us (18%)
  local copies, waits for them, and re-layouts  49.1 us (15%)
  waiting for transfers between devices  30.7 us (9%)
  between operations  30.2 us (9%)
  loops' own time  5.25 us (2%)
    psum x6, blocking collectives, body(): lax.psum((jnp.sum(forward_gap * forward_gap), jnp.sum(backward_gap * back...  85.8 us
    ppermute x12, starting transfers between devices, shifted(): return lax.ppermute(block, axis, route)  39 us
    reduce_sum x48, other arithmetic, force_cells(): jnp.sum((weight * coefficient)[:, None] * separation, axis=-1)  23.9 us
    ppermute x12, waiting for transfers between devices, extended_2(): lax.ppermute(tail, axis, [(i, (i + 1) % count) for i in range(count)])  22.9 us
    ppermute x12, starting transfers between devices, extended_2(): lax.ppermute(head, axis, [((i + 1) % count, i) for i in range(count)])  18.8 us
    reduce_sum x48, other arithmetic, density_cells(): density = density + jnp.sum(weight * remain ** 4, axis=-1)  12.8 us
    slice x48, local copies, waits for them, and re-layouts, tile_weight(): self_tile[:, partner, None, None] & diagonal[None]  12.1 us
    slice x48, local copies, waits for them, and re-layouts, tile_weight(): tile_live[:, partner, None, None]  12 us
  transfers between devices with their start and end apart: 36, of which 13 were waited for; matrix products, arithmetic and copies ran while one was open for 30% of the time, Pallas kernels for 0%

commit v1 on v0

v1 whole, which is shorter than its diff:
```python
import functools

import jax
import jax.numpy as jnp
from jax import lax
from jax.experimental import pallas as pl
from jax.experimental.pallas import tpu as pltpu
from jax.sharding import PartitionSpec as P

LANES = 128
GHOST = 2
ITERATIONS = 6
RADIUS = 3.0
STEP = 0.02
EPS = 1e-6
FAR = 1.0e4
SPAN = 2 * GHOST + 1
ROWS = 32
ONES = 21
PROWS = 8


def parts(v):
    high = v.astype(jnp.bfloat16).astype(jnp.float32)
    rest = v - high
    mid = rest.astype(jnp.bfloat16).astype(jnp.float32)
    return high, mid, rest - mid


def fold(v):
    return jnp.sum(v, axis=(0, 1))[None]


def kernel(
    n, ni, cells,
    data, out,
    wide, live_wide, left_rows, right_rows, pleft, pright,
    flat, turned, pturned, tiles, density, moment,
    halo, usend, urecv, gsend, grecv, fsend, frecv, asend, arecv, bsend, brecv,
    hs, hr, us, ur, gs, gr, fs, fr, as_, ar, bs, br,
):
    ext = 3 * cells
    me = lax.axis_index("space")
    im = lax.axis_index("image")
    right, left = lax.rem(me + 1, n), lax.rem(me + n - 1, n)
    down, up = lax.rem(im + 1, ni), lax.rem(im + ni - 1, ni)

    def sp(d):
        return {"space": d}

    barrier = pltpu.get_barrier_semaphore()
    for d in range(1, n):
        pl.semaphore_signal(barrier, inc=1, device_id=sp(lax.rem(me + d, n)))
    for d in (up, down):
        pl.semaphore_signal(barrier, inc=1, device_id={"image": d})
    pl.semaphore_wait(barrier, n + 1)

    def remote(src, dst, ssem, rsem, dev):
        return pltpu.make_async_remote_copy(
            src_ref=src, dst_ref=dst, send_sem=ssem, recv_sem=rsem,
            device_id=dev, device_id_type=pl.DeviceIdType.MESH,
        )

    first = [
        remote(data.at[pl.ds(0, 5)], halo.at[0], hs.at[0], hr.at[0], sp(right)),
        remote(data.at[pl.ds(0, 5)], halo.at[1], hs.at[1], hr.at[1], sp(left)),
    ]
    for c in first:
        c.start()

    cell_id = lax.broadcasted_iota(jnp.int32, (ext, LANES), 0)
    slot = lax.broadcasted_iota(jnp.int32, (ext, LANES), 1)
    site = [
        (slot // 64 + 2 * cell_id - ext).astype(jnp.float32),
        (slot // 8 % 8).astype(jnp.float32) - 3.5,
        (slot % 8).astype(jnp.float32) - 3.5,
    ]
    one = jnp.ones((ext, LANES), jnp.float32)
    zero = jnp.zeros((ext, LANES), jnp.float32)

    def put(ref, row, v):
        ref[pl.ds(row * ext, ext), :] = v

    for r in range(3):
        put(left_rows, ONES + r, one)
        put(right_rows, ONES - 3 + r, one)
    for r in range(ONES + 3 + SPAN, ROWS):
        put(left_rows, r, zero)
        put(right_rows, r, zero)
    for r in range(PROWS):
        put(pleft, r, one if 3 <= r < 6 else zero)
        put(pright, r, one if r < 3 else zero)
    for r in range(SPAN):
        put(left_rows, ONES + 3 + r, jnp.where(cell_id % SPAN == r, one, zero))
    density[...] = zero
    for c in first:
        c.wait()
    for k in range(3):
        wide[k, pl.ds(0, cells), :] = halo[0, k]
        wide[k, pl.ds(cells, cells), :] = data[k]
        wide[k, pl.ds(2 * cells, cells), :] = halo[1, k]
    live_wide[pl.ds(0, cells), :] = halo[0, 3]
    live_wide[pl.ds(cells, cells), :] = data[3]
    live_wide[pl.ds(2 * cells, cells), :] = halo[1, 3]
    used = jnp.concatenate([halo[0, 4], data[4], halo[1, 4]], axis=0)
    bars = [
        jnp.broadcast_to((used[:, o : o + 1] - 1.0) * FAR, (ext, LANES)) for o in range(SPAN)
    ]
    for r in range(SPAN):
        bar = zero
        for o in range(SPAN):
            bar = jnp.where((cell_id + (o + SPAN - GHOST)) % SPAN == r, bars[o], bar)
        put(right_rows, ONES + 3 + r, bar)

    low = cells - 2 * GHOST
    diagonal = lax.broadcasted_iota(jnp.int32, (LANES, LANES), 0) == lax.broadcasted_iota(
        jnp.int32, (LANES, LANES), 1
    )
    spring_const = data[11]
    own = pl.ds(cells, cells)

    def step(it, carry):
        par = lax.rem(it, 2)
        for k in range(3):
            usend[par, k] = wide[k, own, :]
        ucopy = [
            remote(usend.at[par], urecv.at[par, 0], us.at[par, 0], ur.at[par, 0], {"image": down}),
            remote(usend.at[par], urecv.at[par, 1], us.at[par, 1], ur.at[par, 1], {"image": up}),
        ]
        for c in ucopy:
            c.start()

        live = live_wide[...]
        place = [(wide[k] + site[k]) * (1.0 / RADIUS) for k in range(3)]
        for k in range(3):
            h, m, l = parts(place[k])
            for j, v in enumerate((h, h, m, m, h, l)):
                put(left_rows, 6 * k + j, v)
            h, m, l = 2.0 * h, 2.0 * m, 2.0 * l
            for j, v in enumerate((h, m, h, m, l, h)):
                put(right_rows, 6 * k + j, v)
        square = place[0] * place[0] + place[1] * place[1] + place[2] * place[2]
        q = 0.5 - square + (live - 1.0) * FAR
        for j, v in enumerate(parts(q)):
            put(left_rows, ONES - 3 + j, v)
            put(right_rows, ONES + j, v)

        for e in range(low, ext - low):
            block = left_rows[pl.ds(e, ROWS, stride=ext), :]
            flat[:, pl.ds(e * LANES, LANES)] = block.astype(jnp.bfloat16)
            turned[pl.ds((e - low) * LANES, LANES), :] = block.T.astype(jnp.bfloat16)

        for c in range(cells - GHOST, 2 * cells + GHOST):
            near = right_rows[pl.ds(c, ROWS, stride=ext), :].astype(jnp.bfloat16)
            t = jnp.dot(
                turned[pl.ds((c - GHOST - low) * LANES, SPAN * LANES), :], near,
                preferred_element_type=jnp.float32,
            )
            t = jnp.maximum(t, 0.0)
            a, b = GHOST * LANES, (GHOST + 1) * LANES
            t = jnp.concatenate([t[:a], jnp.where(diagonal, 0.0, t[a:b]), t[b:]], axis=0)
            if cells <= c < 2 * cells:
                tiles[c - cells] = t
            s = t * t
            s = s * s
            density[pl.ds(c, 1), :] = jnp.sum(s, axis=0, keepdims=True)

        for c in ucopy:
            c.wait_recv()
        own_live = live_wide[own, :]
        ahead, behind = [], []
        for k in range(3):
            mine = wide[k, own, :]
            prev = jnp.where(im == 0, data[5 + k], urecv[par, 0, k])
            nxt = jnp.where(im == ni - 1, data[8 + k], urecv[par, 1, k])
            ahead.append((nxt - mine) * own_live)
            behind.append((mine - prev) * own_live)
            gsend[par, k] = ahead[k]
            gsend[par, 3 + k] = behind[k]
        gcopy = [
            remote(gsend.at[par], grecv.at[par, 0], gs.at[par, 0], gr.at[par, 0], sp(right)),
            remote(gsend.at[par], grecv.at[par, 1], gs.at[par, 1], gr.at[par, 1], sp(left)),
        ]
        for c in gcopy:
            c.start()

        def lanes(x, y):
            v = x[0] * y[0] + x[1] * y[1] + x[2] * y[2]
            return jnp.sum(v, axis=0, keepdims=True)

        def spread(send, recv, ssem, rsem, rows):
            for j, v in enumerate(rows):
                send[par, pl.ds(j, 1), :] = v
                recv[par, me, pl.ds(j, 1), :] = v
            copies = []
            for d in range(1, n):
                copies.append(
                    remote(
                        send.at[par], recv.at[par, me], ssem.at[par, d], rsem.at[par, d],
                        sp(lax.rem(me + d, n)),
                    )
                )
                copies[-1].start()
            return copies

        acopy = spread(
            asend, arecv, as_, ar,
            [lanes(ahead, ahead), lanes(behind, behind), lanes(ahead, behind), own_live[:1]],
        )

        steep = 2.0 * live / jnp.sqrt(1.0 + density[...])
        for j, v in enumerate(parts(steep)):
            put(pleft, j, v)
            put(pright, 3 + j, v)
        for e in range(cells - GHOST, 2 * cells + GHOST):
            block = pleft[pl.ds(e, PROWS, stride=ext), :]
            pturned[pl.ds((e - cells + GHOST) * LANES, LANES), :] = block.T.astype(jnp.bfloat16)
        for c in range(cells):
            near = pright[pl.ds(c + cells, PROWS, stride=ext), :].astype(jnp.bfloat16)
            both = jnp.dot(
                pturned[pl.ds(c * LANES, SPAN * LANES), :], near,
                preferred_element_type=jnp.float32,
            )
            t = tiles[c]
            pull = (t * t) * (both * t - 1.2)
            high = pull.astype(jnp.bfloat16)
            rest = (pull - high.astype(jnp.float32)).astype(jnp.bfloat16)
            x = flat[:, pl.ds((c + cells - GHOST) * LANES, SPAN * LANES)]
            v = jnp.dot(x, high, preferred_element_type=jnp.float32) + jnp.dot(
                x, rest, preferred_element_type=jnp.float32
            )
            for k in range(3):
                moment[k, pl.ds(c, 1), :] = (
                    v[6 * k : 6 * k + 1] + v[6 * k + 2 : 6 * k + 3] + v[6 * k + 5 : 6 * k + 6]
                )
            moment[3, pl.ds(c, 1), :] = v[ONES : ONES + 1]

        total = moment[3]
        force = [
            (moment[k] - place[k][cells : 2 * cells] * total) * (2.0 / RADIUS) for k in range(3)
        ]
        for k in range(3):
            fsend[par, k] = force[k]
        bcopy = spread(bsend, brecv, bs, br, [lanes(force, ahead), lanes(force, behind)])
        fcopy = [
            remote(fsend.at[par], frecv.at[par, 0], fs.at[par, 0], fr.at[par, 0], sp(right)),
            remote(fsend.at[par], frecv.at[par, 1], fs.at[par, 1], fr.at[par, 1], sp(left)),
        ]
        for c in fcopy:
            c.start()

        for c in acopy:
            c.wait_recv()
        sums = jnp.sum(jnp.sum(arecv[par], axis=0), axis=-1, keepdims=True)
        aa, bb, ab = sums[0:1], sums[1:2], sums[2:3]
        la, lb = jnp.sqrt(aa + EPS), jnp.sqrt(bb + EPS)
        cosine = ab / (la * lb)
        norm = jnp.sqrt(jnp.maximum(aa / (la * la) + bb / (lb * lb) + 2.0 * cosine, 1.0))
        ga, gb = 1.0 / (la * norm), 1.0 / (lb * norm)
        spring = spring_const[0:1] * (la - lb)
        for c in gcopy:
            c.wait_recv()
        for c in fcopy:
            c.wait_recv()
        for c in bcopy:
            c.wait_recv()
        sums = jnp.sum(jnp.sum(brecv[par], axis=0), axis=-1, keepdims=True)
        parallel = sums[0:1] * ga + sums[1:2] * gb
        gain = spring - parallel
        ga, gb = gain * ga, gain * gb
        for k in range(3):
            band = force[k] + (ahead[k] * ga + behind[k] * gb)
            out[k] = band
            wide[k, own, :] = wide[k, own, :] + STEP * band
            for side in range(2):
                where = pl.ds(2 * cells * side, cells)
                band = frecv[par, side, k] + (
                    grecv[par, side, k] * ga + grecv[par, side, 3 + k] * gb
                )
                wide[k, where, :] = wide[k, where, :] + STEP * band
        out[3, pl.ds(0, 1), :] = jnp.broadcast_to(parallel, (1, LANES))
        out[3, pl.ds(1, 1), :] = jnp.broadcast_to(spring, (1, LANES))
        out[3, pl.ds(2, 1), :] = jnp.broadcast_to(cosine, (1, LANES))
        for c in ucopy + gcopy + acopy + bcopy + fcopy:
            c.wait_send()
        return carry

    out[3] = jnp.zeros((cells, LANES), jnp.float32)
    lax.fori_loop(0, ITERATIONS, step, 0)


def solution(mesh):
    n, ni = mesh.shape["space"], mesh.shape["image"]

    def body(displacement, end_states, atom_live, partner_cells, partner_live, spring_const):
        cells = partner_cells.shape[0]
        own = jnp.arange(cells, dtype=jnp.int32)[:, None, None]
        offset = jnp.arange(LANES, dtype=jnp.int32)[None, None, :]
        hit = (partner_cells[:, :, None] == own + offset) & (partner_live[:, :, None] > 0)
        used = jnp.any(hit, axis=1).astype(jnp.float32)
        data = jnp.concatenate(
            [
                displacement.reshape(3, cells, LANES),
                atom_live.astype(jnp.float32).reshape(1, cells, LANES),
                used[None],
                end_states.reshape(6, cells, LANES),
                jnp.broadcast_to(spring_const[:, None, None], (1, cells, LANES)),
            ],
            axis=0,
        )
        ext = 3 * cells
        f32, bf16 = jnp.float32, jnp.bfloat16
        sem = pltpu.SemaphoreType.DMA
        V = pltpu.VMEM
        inner = cells + 2 * GHOST
        out = pl.pallas_call(
            functools.partial(kernel, n, ni, cells),
            out_shape=jax.ShapeDtypeStruct((4, cells, LANES), f32),
            in_specs=[pl.BlockSpec(memory_space=pltpu.VMEM)],
            out_specs=pl.BlockSpec(memory_space=pltpu.VMEM),
            scratch_shapes=[
                V((3, ext, LANES), f32),
                V((ext, LANES), f32),
                V((ROWS * ext, LANES), f32),
                V((ROWS * ext, LANES), f32),
                V((PROWS * ext, LANES), f32),
                V((PROWS * ext, LANES), f32),
                V((ROWS, ext * LANES), bf16),
                V(((inner + 2 * GHOST) * LANES, ROWS), bf16),
                V((inner * LANES, PROWS), bf16),
                V((cells, SPAN * LANES, LANES), f32),
                V((ext, LANES), f32),
                V((4, cells, LANES), f32),
                V((2, 5, cells, LANES), f32),
                V((2, 3, cells, LANES), f32),
                V((2, 2, 3, cells, LANES), f32),
                V((2, 6, cells, LANES), f32),
                V((2, 2, 6, cells, LANES), f32),
                V((2, 3, cells, LANES), f32),
                V((2, 2, 3, cells, LANES), f32),
                V((2, 4, LANES), f32),
                V((2, n, 4, LANES), f32),
                V((2, 2, LANES), f32),
                V((2, n, 2, LANES), f32),
                sem((2,)), sem((2,)),
                sem((2, 2)), sem((2, 2)),
                sem((2, 2)), sem((2, 2)),
                sem((2, 2)), sem((2, 2)),
                sem((2, n)), sem((2, n)),
                sem((2, n)), sem((2, n)),
            ],
            compiler_params=pltpu.CompilerParams(collective_id=0, has_side_effects=True),
        )(data)
        return out[:3].reshape(1, 3, -1), out[3, :3, 0][None]

    return jax.shard_map(
        body,
        mesh=mesh,
        in_specs=(
            P("image", None, "space"),
            P(None, None, "space"),
            P("space"),
            P("space", None),
            P("space", None),
            P("image"),
        ),
        out_specs=(P("image", None, "space"), P("image", None)),
        check_vma=False,
    )
```

time: 332 us -> 69.2 us (0.21)
  blocking collectives: 85.8 us -> 0 us
  other arithmetic: 68.9 us -> 0.1 us
  Pallas kernels: 0 us -> 62.8 us
  starting transfers between devices: 60.3 us -> 0 us
  local copies, waits for them, and re-layouts: 49.1 us -> 4.6 us
  waiting for transfers between devices: 30.7 us -> 0 us
  between operations: 30.2 us -> 1.37 us
  loops' own time: 5.25 us -> 0 us
    psum x6 -> x0, blocking collectives: 85.8 us -> none  [body(): lax.psum((jnp.sum(forward_gap * forward_gap), jnp.sum(backward_gap * back...]
    pallas_call x0 -> x1, Pallas kernels: none -> 62.8 us  [body(): pl.pallas_call(functools.partial(kernel, n, ni, cells), out_shape=jax.Sha...]
    ppermute x36 -> x0, starting transfers between devices: 60.3 us -> none  [the longest x12 39 us: shifted(): return lax.ppermute(block, axis, route)]
    reduce_sum x156 -> x0, other arithmetic: 55.2 us -> none  [the longest x48 23.9 us: force_cells(): jnp.sum((weight * coefficient)[:, None] * separation, axis=-1)]
    ppermute x36 -> x0, waiting for transfers between devices: 30.7 us -> none  [the longest x12 22.9 us: extended_2(): lax.ppermute(tail, axis, [(i, (i + 1) % count) for i in range(count)])]
    slice x121 -> x2, local copies, waits for them, and re-layouts: 28.4 us -> 2.61 us  [body(): return (out[:3].reshape(1, 3, -1), out[3, :3, 0][None])]
    mul x85 -> x0, other arithmetic: 11 us -> none  [the longest x48 10.6 us: force_cells(): weight * coefficient]
    gather x18 -> x0, local copies, waits for them, and re-layouts: 10.7 us -> none  [the longest x6 3.72 us: body(): partner_sites = placed[:, partner_cells].transpose(1, 2, 0, 3)]
  transfers between devices with their start and end apart: 36 -> 0, of which waited for: 13 -> 0; matrix products, arithmetic and copies ran while one was open for 30% -> 0% of each run, Pallas kernels for 0% -> 0%
where the time goes in v1:
time: 69.2 us; the launch traced here: 68.9 us
  Pallas kernels  62.8 us (91%)
  local copies, waits for them, and re-layouts  4.6 us (7%)
  between operations  1.37 us (2%)
    pallas_call x1, Pallas kernels, body(): pl.pallas_call(functools.partial(kernel, n, ni, cells), out_shape=jax.Sha...  62.8 us
    slice x2, local copies, waits for them, and re-layouts, body(): return (out[:3].reshape(1, 3, -1), out[3, :3, 0][None])  2.61 us
    unnamed x14, local copies, waits for them, and re-layouts  1.88 us

profile of v1, /device:TPU:0, one launch (start us, length us, event | category | flops | bytes accessed | tf_op | source)
XLA Modules:
  0.0 68.9 jit_solution(15509074644312276912)
XLA Ops:
  0.6 0.0 copy-start.3
  0.6 0.0 copy-start.4
  0.7 0.0 copy-start.2
  0.7 0.7 %constant_dynamic-update-slice_fusion.4 = f32[12,8,128]{2,1,0:T(8,128)S(1)} fusion(f32[3,8,128]{2,1,0:T(8,128)} %bitcast.9), kind=kLoop, calls=%fused_computation.5 | loop fusion | bytes 24576
  1.4 0.0 copy-done.3
  1.4 0.0 copy-start.1
  1.4 0.0 copy-done.4
  1.4 0.1 copy.12
  1.5 0.0 copy-done.2
  1.5 0.1 copy.13
  1.6 0.1 and_reduce_fusion
  1.7 0.4 copy-done.1
  2.8 0.0 copy-start
  2.8 0.6 copy-done
  3.5 62.8 %shard_map.77 = f32[4,8,128]{2,1,0:T(8,128)} custom-call(f32[12,8,128]{2,1,0:T(8,128)} %copy-done), custom_call_target="tpu_custom_call" | custom-call | tf_op jit(solution)/shard_map/pallas_call | solution.py:316
  66.2 1.3 %slice.6 = f32[3,8,128]{2,1,0:T(8,128)} slice(f32[4,8,128]{2,1,0:T(8,128)} %shard_map.77), slice={[0:3], [0:8], [0:128]} | slice | bytes 24576 | tf_op jit(solution)/shard_map/slice | solution.py:354
  67.6 1.3 %slice_reduce_fusion = f32[3]{0:T(128)} fusion(f32[4,8,128]{2,1,0:T(8,128)} %shard_map.77), kind=kLoop, calls=%fused_computation.7 | loop fusion | bytes 24 | tf_op jit(solution)/shard_map/slice | solution.py:354
  (8 shorter events, 0.1 us)
Async XLA Ops:
  0.6 0.8 %copy-start.3 = (s32[1024]{0:T(1024)S(1)}, s32[1024]{0:T(1024)}, u32[]{:S(2)}) copy-start(s32[1024]{0:T(1024)} %param.8) | copy-start | bytes 12292
  0.6 0.8 %copy-start.4 = (s32[8,5]{1,0:T(8,128)S(1)}, s32[8,5]{1,0:T(8,128)}, u32[]{:S(2)}) copy-start(s32[8,5]{1,0:T(8,128)} %param.9) | copy-start | bytes 484
  0.7 0.8 %copy-start.2 = (s32[8,5]{1,0:T(8,128)S(1)}, s32[8,5]{1,0:T(8,128)}, u32[]{:S(2)}) copy-start(s32[8,5]{1,0:T(8,128)} %param.10) | copy-start | bytes 484
  1.4 0.7 %copy-start.1 = (f32[2,3,1024]{2,0,1:T(2,128)S(1)}, f32[2,3,1024]{2,0,1:T(2,128)}, u32[]{:S(2)}) copy-start(f32[2,3,1024]{2,0,1:T(2,128)} %param.7) | copy-start | bytes 73732
  2.8 0.6 copy-start

commit v2 on v1

--- a/solution.py
+++ b/solution.py
@@ -53,7 +53,6 @@
         pl.semaphore_signal(barrier, inc=1, device_id=sp(lax.rem(me + d, n)))
     for d in (up, down):
         pl.semaphore_signal(barrier, inc=1, device_id={"image": d})
-    pl.semaphore_wait(barrier, n + 1)
 
     def remote(src, dst, ssem, rsem, dev):
         return pltpu.make_async_remote_copy(
@@ -65,8 +64,6 @@
         remote(data.at[pl.ds(0, 5)], halo.at[0], hs.at[0], hr.at[0], sp(right)),
         remote(data.at[pl.ds(0, 5)], halo.at[1], hs.at[1], hr.at[1], sp(left)),
     ]
-    for c in first:
-        c.start()
 
     cell_id = lax.broadcasted_iota(jnp.int32, (ext, LANES), 0)
     slot = lax.broadcasted_iota(jnp.int32, (ext, LANES), 1)
@@ -93,6 +90,9 @@
     for r in range(SPAN):
         put(left_rows, ONES + 3 + r, jnp.where(cell_id % SPAN == r, one, zero))
     density[...] = zero
+    pl.semaphore_wait(barrier, n + 1)
+    for c in first:
+        c.start()
     for c in first:
         c.wait()
     for k in range(3):
@@ -165,25 +165,6 @@
             s = s * s
             density[pl.ds(c, 1), :] = jnp.sum(s, axis=0, keepdims=True)
 
-        for c in ucopy:
-            c.wait_recv()
-        own_live = live_wide[own, :]
-        ahead, behind = [], []
-        for k in range(3):
-            mine = wide[k, own, :]
-            prev = jnp.where(im == 0, data[5 + k], urecv[par, 0, k])
-            nxt = jnp.where(im == ni - 1, data[8 + k], urecv[par, 1, k])
-            ahead.append((nxt - mine) * own_live)
-            behind.append((mine - prev) * own_live)
-            gsend[par, k] = ahead[k]
-            gsend[par, 3 + k] = behind[k]
-        gcopy = [
-            remote(gsend.at[par], grecv.at[par, 0], gs.at[par, 0], gr.at[par, 0], sp(right)),
-            remote(gsend.at[par], grecv.at[par, 1], gs.at[par, 1], gr.at[par, 1], sp(left)),
-        ]
-        for c in gcopy:
-            c.start()
-
         def lanes(x, y):
             v = x[0] * y[0] + x[1] * y[1] + x[2] * y[2]
             return jnp.sum(v, axis=0, keepdims=True)
@@ -203,11 +184,6 @@
                 copies[-1].start()
             return copies
 
-        acopy = spread(
-            asend, arecv, as_, ar,
-            [lanes(ahead, ahead), lanes(behind, behind), lanes(ahead, behind), own_live[:1]],
-        )
-
         steep = 2.0 * live / jnp.sqrt(1.0 + density[...])
         for j, v in enumerate(parts(steep)):
             put(pleft, j, v)
@@ -216,6 +192,30 @@
             block = pleft[pl.ds(e, PROWS, stride=ext), :]
             pturned[pl.ds((e - cells + GHOST) * LANES, LANES), :] = block.T.astype(jnp.bfloat16)
         for c in range(cells):
+            if c == cells - 2:
+                for copy in ucopy:
+                    copy.wait_recv()
+                own_live = live_wide[own, :]
+                ahead, behind = [], []
+                for k in range(3):
+                    mine = wide[k, own, :]
+                    prev = jnp.where(im == 0, data[5 + k], urecv[par, 0, k])
+                    nxt = jnp.where(im == ni - 1, data[8 + k], urecv[par, 1, k])
+                    ahead.append((nxt - mine) * own_live)
+                    behind.append((mine - prev) * own_live)
+                    gsend[par, k] = ahead[k]
+                    gsend[par, 3 + k] = behind[k]
+                gcopy = [
+                    remote(gsend.at[par], grecv.at[par, 0], gs.at[par, 0], gr.at[par, 0], sp(right)),
+                    remote(gsend.at[par], grecv.at[par, 1], gs.at[par, 1], gr.at[par, 1], sp(left)),
+                ]
+                for copy in gcopy:
+                    copy.start()
+
+                acopy = spread(
+                    asend, arecv, as_, ar,
+                    [lanes(ahead, ahead), lanes(behind, behind), lanes(ahead, behind), own_live[:1]],
+                )
             near = pright[pl.ds(c + cells, PROWS, stride=ext), :].astype(jnp.bfloat16)
             both = jnp.dot(
                 pturned[pl.ds(c * LANES, SPAN * LANES), :], near,

time: 69.2 us -> 62.3 us (0.900)
  Pallas kernels: 62.8 us -> 55.8 us
    pallas_call x1, Pallas kernels: 62.8 us -> 55.8 us  [body(): pl.pallas_call(functools.partial(kernel, n, ni, cells), out_shape=jax.Sha...]
where the time goes in v2:
time: 62.3 us; the launch traced here: 61.9 us
  Pallas kernels  55.8 us (90%)
  local copies, waits for them, and re-layouts  4.6 us (7%)
  between operations  1.37 us (2%)
    pallas_call x1, Pallas kernels, body(): pl.pallas_call(functools.partial(kernel, n, ni, cells), out_shape=jax.Sha...  55.8 us
    slice x2, local copies, waits for them, and re-layouts, body(): return (out[:3].reshape(1, 3, -1), out[3, :3, 0][None])  2.61 us
    unnamed x14, local copies, waits for them, and re-layouts  1.88 us

profile of v2, /device:TPU:0, one launch (start us, length us, event | category | flops | bytes accessed | tf_op | source)
XLA Modules:
  0.0 61.9 jit_solution(9105503279229752796)
XLA Ops:
  0.6 0.0 copy-start.3
  0.6 0.0 copy-start.4
  0.7 0.0 copy-start.2
  0.7 0.7 %constant_dynamic-update-slice_fusion.4 = f32[12,8,128]{2,1,0:T(8,128)S(1)} fusion(f32[3,8,128]{2,1,0:T(8,128)} %bitcast.9), kind=kLoop, calls=%fused_computation.5 | loop fusion | bytes 24576
  1.4 0.0 copy-done.3
  1.4 0.0 copy-start.1
  1.4 0.0 copy-done.4
  1.4 0.1 copy.12
  1.5 0.0 copy-done.2
  1.5 0.1 copy.13
  1.6 0.1 and_reduce_fusion
  1.7 0.4 copy-done.1
  2.8 0.0 copy-start
  2.8 0.6 copy-done
  3.5 55.8 %shard_map.77 = f32[4,8,128]{2,1,0:T(8,128)} custom-call(f32[12,8,128]{2,1,0:T(8,128)} %copy-done), custom_call_target="tpu_custom_call" | custom-call | tf_op jit(solution)/shard_map/pallas_call | solution.py:316
  59.3 1.3 %slice.6 = f32[3,8,128]{2,1,0:T(8,128)} slice(f32[4,8,128]{2,1,0:T(8,128)} %shard_map.77), slice={[0:3], [0:8], [0:128]} | slice | bytes 24576 | tf_op jit(solution)/shard_map/slice | solution.py:354
  60.6 1.3 %slice_reduce_fusion = f32[3]{0:T(128)} fusion(f32[4,8,128]{2,1,0:T(8,128)} %shard_map.77), kind=kLoop, calls=%fused_computation.7 | loop fusion | bytes 24 | tf_op jit(solution)/shard_map/slice | solution.py:354
  (8 shorter events, 0.1 us)
Async XLA Ops:
  0.6 0.8 %copy-start.3 = (s32[1024]{0:T(1024)S(1)}, s32[1024]{0:T(1024)}, u32[]{:S(2)}) copy-start(s32[1024]{0:T(1024)} %param.8) | copy-start | bytes 12292
  0.6 0.8 %copy-start.4 = (s32[8,5]{1,0:T(8,128)S(1)}, s32[8,5]{1,0:T(8,128)}, u32[]{:S(2)}) copy-start(s32[8,5]{1,0:T(8,128)} %param.9) | copy-start | bytes 484
  0.7 0.8 %copy-start.2 = (s32[8,5]{1,0:T(8,128)S(1)}, s32[8,5]{1,0:T(8,128)}, u32[]{:S(2)}) copy-start(s32[8,5]{1,0:T(8,128)} %param.10) | copy-start | bytes 484
  1.4 0.7 %copy-start.1 = (f32[2,3,1024]{2,0,1:T(2,128)S(1)}, f32[2,3,1024]{2,0,1:T(2,128)}, u32[]{:S(2)}) copy-start(f32[2,3,1024]{2,0,1:T(2,128)} %param.7) | copy-start | bytes 73732
  2.8 0.6 %copy-start = (f32[12,8,128]{2,1,0:T(8,128)}, f32[12,8,128]{2,1,0:T(8,128)S(1)}, u32[]{:S(2)}) copy-start(f32[12,8,128]{2,1,0:T(8,128)S(1)} %constant_dynamic-update-slice_fusion.data) | copy-start | bytes 147460

commit v3 on v2

--- a/solution.py
+++ b/solution.py
@@ -33,7 +33,8 @@
 
 def kernel(
     n, ni, cells,
-    data, out,
+    disp, ends, atoms, pcells, plive, spring_ref, out, stats,
+    data,
     wide, live_wide, left_rows, right_rows, pleft, pright,
     flat, turned, pturned, tiles, density, moment,
     halo, usend, urecv, gsend, grecv, fsend, frecv, asend, arecv, bsend, brecv,
@@ -59,6 +60,19 @@
             src_ref=src, dst_ref=dst, send_sem=ssem, recv_sem=rsem,
             device_id=dev, device_id_type=pl.DeviceIdType.MESH,
         )
+
+    for k in range(3):
+        data[k] = disp[k]
+        data[5 + k] = ends[k, pl.ds(0, cells, stride=2), :]
+        data[8 + k] = ends[k, pl.ds(1, cells, stride=2), :]
+    data[3] = atoms[...].astype(jnp.float32)
+    lane = lax.broadcasted_iota(jnp.int32, (cells, LANES), 1)
+    base = lax.broadcasted_iota(jnp.int32, (cells, SPAN), 0)
+    use = jnp.zeros((cells, LANES), jnp.float32)
+    for o in range(SPAN):
+        hit = jnp.where((pcells[...] == base + o) & (plive[...] > 0), 1.0, 0.0)
+        use = jnp.where(lane == o, jnp.max(hit, axis=1, keepdims=True), use)
+    data[4] = use
 
     first = [
         remote(data.at[pl.ds(0, 5)], halo.at[0], hs.at[0], hr.at[0], sp(right)),
@@ -116,7 +130,7 @@
     diagonal = lax.broadcasted_iota(jnp.int32, (LANES, LANES), 0) == lax.broadcasted_iota(
         jnp.int32, (LANES, LANES), 1
     )
-    spring_const = data[11]
+    spring_const = spring_ref[0]
     own = pl.ds(cells, cells)
 
     def step(it, carry):
@@ -257,7 +271,7 @@
         cosine = ab / (la * lb)
         norm = jnp.sqrt(jnp.maximum(aa / (la * la) + bb / (lb * lb) + 2.0 * cosine, 1.0))
         ga, gb = 1.0 / (la * norm), 1.0 / (lb * norm)
-        spring = spring_const[0:1] * (la - lb)
+        spring = spring_const * (la - lb)
         for c in gcopy:
             c.wait_recv()
         for c in fcopy:
@@ -278,14 +292,13 @@
                     grecv[par, side, k] * ga + grecv[par, side, 3 + k] * gb
                 )
                 wide[k, where, :] = wide[k, where, :] + STEP * band
-        out[3, pl.ds(0, 1), :] = jnp.broadcast_to(parallel, (1, LANES))
-        out[3, pl.ds(1, 1), :] = jnp.broadcast_to(spring, (1, LANES))
-        out[3, pl.ds(2, 1), :] = jnp.broadcast_to(cosine, (1, LANES))
+        stats[:, 0:1] = parallel
+        stats[:, 1:2] = spring
+        stats[:, 2:3] = cosine
         for c in ucopy + gcopy + acopy + bcopy + fcopy:
             c.wait_send()
         return carry
 
-    out[3] = jnp.zeros((cells, LANES), jnp.float32)
     lax.fori_loop(0, ITERATIONS, step, 0)
 
 
@@ -294,31 +307,22 @@
 
     def body(displacement, end_states, atom_live, partner_cells, partner_live, spring_const):
         cells = partner_cells.shape[0]
-        own = jnp.arange(cells, dtype=jnp.int32)[:, None, None]
-        offset = jnp.arange(LANES, dtype=jnp.int32)[None, None, :]
-        hit = (partner_cells[:, :, None] == own + offset) & (partner_live[:, :, None] > 0)
-        used = jnp.any(hit, axis=1).astype(jnp.float32)
-        data = jnp.concatenate(
-            [
-                displacement.reshape(3, cells, LANES),
-                atom_live.astype(jnp.float32).reshape(1, cells, LANES),
-                used[None],
-                end_states.reshape(6, cells, LANES),
-                jnp.broadcast_to(spring_const[:, None, None], (1, cells, LANES)),
-            ],
-            axis=0,
-        )
         ext = 3 * cells
         f32, bf16 = jnp.float32, jnp.bfloat16
         sem = pltpu.SemaphoreType.DMA
         V = pltpu.VMEM
         inner = cells + 2 * GHOST
-        out = pl.pallas_call(
+        band, stats = pl.pallas_call(
             functools.partial(kernel, n, ni, cells),
-            out_shape=jax.ShapeDtypeStruct((4, cells, LANES), f32),
-            in_specs=[pl.BlockSpec(memory_space=pltpu.VMEM)],
-            out_specs=pl.BlockSpec(memory_space=pltpu.VMEM),
+            out_shape=(
+                jax.ShapeDtypeStruct((3, cells, LANES), f32),
+                jax.ShapeDtypeStruct((1, 3), f32),
+            ),
+            in_specs=[pl.BlockSpec(memory_space=pltpu.VMEM)] * 5
+            + [pl.BlockSpec(memory_space=pltpu.SMEM)],
+            out_specs=(pl.BlockSpec(memory_space=pltpu.VMEM),) * 2,
             scratch_shapes=[
+                V((11, cells, LANES), f32),
                 V((3, ext, LANES), f32),
                 V((ext, LANES), f32),
                 V((ROWS * ext, LANES), f32),
@@ -350,8 +354,13 @@
                 sem((2, n)), sem((2, n)),
             ],
             compiler_params=pltpu.CompilerParams(collective_id=0, has_side_effects=True),
-        )(data)
-        return out[:3].reshape(1, 3, -1), out[3, :3, 0][None]
+        )(
+            displacement.reshape(3, cells, LANES),
+            end_states.reshape(2, 3, cells, LANES).transpose(1, 2, 0, 3).reshape(3, -1, LANES),
+            atom_live.reshape(cells, LANES),
+            partner_cells, partner_live, spring_const,
+        )
+        return band.reshape(1, 3, -1), stats
 
     return jax.shard_map(
         body,

time: 62.3 us -> 58.9 us (0.945)
  local copies, waits for them, and re-layouts: 4.6 us -> 1.82 us
    slice x2 -> x0, local copies, waits for them, and re-layouts: 2.61 us -> none  [body(): return (out[:3].reshape(1, 3, -1), out[3, :3, 0][None])]
    unnamed x14 -> x4, local copies, waits for them, and re-layouts: 1.88 us -> 1.82 us
where the time goes in v3:
time: 58.9 us; the launch traced here: 58.7 us
  Pallas kernels  55.6 us (94%)
  local copies, waits for them, and re-layouts  1.82 us (3%)
  between operations  1.29 us (2%)
    pallas_call x1, Pallas kernels, body(): pl.pallas_call(functools.partial(kernel, n, ni, cells), out_shape=(jax.Sh...  55.6 us
    unnamed x4, local copies, waits for them, and re-layouts  1.82 us

profile of v3, /device:TPU:0, one launch (start us, length us, event | category | flops | bytes accessed | tf_op | source)
XLA Modules:
  0.0 58.7 jit_solution(6161982609892391612)
XLA Ops:
  1.3 55.6 %shard_map.77 = (f32[3,8,128]{2,1,0:T(8,128)}, f32[1,3]{1,0:T(1,128)}) custom-call(f32[3,8,128]{2,1,0:T(8,128)} %bitcast.10, f32[3,16,128]{2,1,0:T(8,128)} %bitcast.8, s32[8,128]{1,0:T(8,128)} %bitcast.11, s32[8,5]{1,0:T(8,128)} %pcells.1, s32[8,5]{1,0:T(8,128)} %plive.1, f32[1]{0:T(128)S(6)} %copy.14.spring_ref), custom_call_target="tpu_custom_call" | custom-call | tf_op jit(solution)/shard_map/pallas_call | solution.py:315
  56.9 0.0 copy-start
  56.9 1.3 %copy.15 = f32[1,3,1024]{2,0,1:T(1,128)} copy(f32[1,3,1024]{2,0,1:T(1,128)} %bitcast.9) | data formatting | bytes 24576
  58.2 0.0 copy-done
  58.2 0.5 copy.16
Async XLA Ops:
  56.9 1.3 %copy-start = (f32[1,3]{1,0:T(1,128)S(1)}, f32[1,3]{1,0:T(1,128)}, u32[]{:S(2)}) copy-start(f32[1,3]{1,0:T(1,128)} %get-tuple-element.13) | copy-start | bytes 40

commit v4 on v3

--- a/solution.py
+++ b/solution.py
@@ -75,8 +75,8 @@
     data[4] = use
 
     first = [
-        remote(data.at[pl.ds(0, 5)], halo.at[0], hs.at[0], hr.at[0], sp(right)),
-        remote(data.at[pl.ds(0, 5)], halo.at[1], hs.at[1], hr.at[1], sp(left)),
+        remote(data, halo.at[0], hs.at[0], hr.at[0], sp(right)),
+        remote(data, halo.at[1], hs.at[1], hr.at[1], sp(left)),
     ]
 
     cell_id = lax.broadcasted_iota(jnp.int32, (ext, LANES), 0)
@@ -141,7 +141,14 @@
             remote(usend.at[par], urecv.at[par, 0], us.at[par, 0], ur.at[par, 0], {"image": down}),
             remote(usend.at[par], urecv.at[par, 1], us.at[par, 1], ur.at[par, 1], {"image": up}),
         ]
-        for c in ucopy:
+        for k in range(3):
+            gsend[par, k] = wide[k, pl.ds(0, cells), :]
+            gsend[par, 3 + k] = wide[k, pl.ds(2 * cells, cells), :]
+        gcopy = [
+            remote(gsend.at[par], grecv.at[par, 0], gs.at[par, 0], gr.at[par, 0], {"image": down}),
+            remote(gsend.at[par], grecv.at[par, 1], gs.at[par, 1], gr.at[par, 1], {"image": up}),
+        ]
+        for c in ucopy + gcopy:
             c.start()
 
         live = live_wide[...]
@@ -206,7 +213,7 @@
             block = pleft[pl.ds(e, PROWS, stride=ext), :]
             pturned[pl.ds((e - cells + GHOST) * LANES, LANES), :] = block.T.astype(jnp.bfloat16)
         for c in range(cells):
-            if c == cells - 2:
+            if c == cells - 1:
                 for copy in ucopy:
                     copy.wait_recv()
                 own_live = live_wide[own, :]
@@ -217,15 +224,6 @@
                     nxt = jnp.where(im == ni - 1, data[8 + k], urecv[par, 1, k])
                     ahead.append((nxt - mine) * own_live)
                     behind.append((mine - prev) * own_live)
-                    gsend[par, k] = ahead[k]
-                    gsend[par, 3 + k] = behind[k]
-                gcopy = [
-                    remote(gsend.at[par], grecv.at[par, 0], gs.at[par, 0], gr.at[par, 0], sp(right)),
-                    remote(gsend.at[par], grecv.at[par, 1], gs.at[par, 1], gr.at[par, 1], sp(left)),
-                ]
-                for copy in gcopy:
-                    copy.start()
-
                 acopy = spread(
                     asend, arecv, as_, ar,
                     [lanes(ahead, ahead), lanes(behind, behind), lanes(ahead, behind), own_live[:1]],
@@ -274,6 +272,15 @@
         spring = spring_const * (la - lb)
         for c in gcopy:
             c.wait_recv()
+        outer = []
+        for side in range(2):
+            where = pl.ds(2 * cells * side, cells)
+            side_live = live_wide[where, :]
+            for k in range(3):
+                mine = wide[k, where, :]
+                prev = jnp.where(im == 0, halo[side, 5 + k], grecv[par, 0, 3 * side + k])
+                nxt = jnp.where(im == ni - 1, halo[side, 8 + k], grecv[par, 1, 3 * side + k])
+                outer.append(((nxt - mine) * side_live, (mine - prev) * side_live))
         for c in fcopy:
             c.wait_recv()
         for c in bcopy:
@@ -288,9 +295,8 @@
             wide[k, own, :] = wide[k, own, :] + STEP * band
             for side in range(2):
                 where = pl.ds(2 * cells * side, cells)
-                band = frecv[par, side, k] + (
-                    grecv[par, side, k] * ga + grecv[par, side, 3 + k] * gb
-                )
+                gap = outer[3 * side + k]
+                band = frecv[par, side, k] + (gap[0] * ga + gap[1] * gb)
                 wide[k, where, :] = wide[k, where, :] + STEP * band
         stats[:, 0:1] = parallel
         stats[:, 1:2] = spring
@@ -335,7 +341,7 @@
                 V((cells, SPAN * LANES, LANES), f32),
                 V((ext, LANES), f32),
                 V((4, cells, LANES), f32),
-                V((2, 5, cells, LANES), f32),
+                V((2, 11, cells, LANES), f32),
                 V((2, 3, cells, LANES), f32),
                 V((2, 2, 3, cells, LANES), f32),
                 V((2, 6, cells, LANES), f32),

time: 58.9 us -> 58.8 us (level)
  no operation moved by 1% of the time
where the time goes in v4:
time: 58.8 us; the launch traced here: 58.5 us
  Pallas kernels  55.4 us (94%)
  local copies, waits for them, and re-layouts  1.82 us (3%)
  between operations  1.29 us (2%)
    pallas_call x1, Pallas kernels, body(): pl.pallas_call(functools.partial(kernel, n, ni, cells), out_shape=(jax.Sh...  55.4 us
    unnamed x4, local copies, waits for them, and re-layouts  1.82 us

profile of v4, /device:TPU:0, one launch (start us, length us, event | category | flops | bytes accessed | tf_op | source)
XLA Modules:
  0.0 58.5 jit_solution(9222045847928777303)
XLA Ops:
  1.3 55.4 %shard_map.77 = (f32[3,8,128]{2,1,0:T(8,128)}, f32[1,3]{1,0:T(1,128)}) custom-call(f32[3,8,128]{2,1,0:T(8,128)} %bitcast.10, f32[3,16,128]{2,1,0:T(8,128)} %bitcast.8, s32[8,128]{1,0:T(8,128)} %bitcast.11, s32[8,5]{1,0:T(8,128)} %pcells.1, s32[8,5]{1,0:T(8,128)} %plive.1, f32[1]{0:T(128)S(6)} %copy.14.spring_ref), custom_call_target="tpu_custom_call" | custom-call | tf_op jit(solution)/shard_map/pallas_call | solution.py:321
  56.7 0.0 copy-start
  56.7 1.3 %copy.15 = f32[1,3,1024]{2,0,1:T(1,128)} copy(f32[1,3,1024]{2,0,1:T(1,128)} %bitcast.9) | data formatting | bytes 24576
  58.0 0.0 copy-done
  58.0 0.5 copy.16
Async XLA Ops:
  56.7 1.3 %copy-start = (f32[1,3]{1,0:T(1,128)S(1)}, f32[1,3]{1,0:T(1,128)}, u32[]{:S(2)}) copy-start(f32[1,3]{1,0:T(1,128)} %get-tuple-element.13) | copy-start | bytes 40

commit v5 on v3

--- a/solution.py
+++ b/solution.py
@@ -206,7 +206,7 @@
             block = pleft[pl.ds(e, PROWS, stride=ext), :]
             pturned[pl.ds((e - cells + GHOST) * LANES, LANES), :] = block.T.astype(jnp.bfloat16)
         for c in range(cells):
-            if c == cells - 2:
+            if c == cells - 1:
                 for copy in ucopy:
                     copy.wait_recv()
                 own_live = live_wide[own, :]
@@ -223,13 +223,13 @@
                     remote(gsend.at[par], grecv.at[par, 0], gs.at[par, 0], gr.at[par, 0], sp(right)),
                     remote(gsend.at[par], grecv.at[par, 1], gs.at[par, 1], gr.at[par, 1], sp(left)),
                 ]
-                for copy in gcopy:
-                    copy.start()
 
                 acopy = spread(
                     asend, arecv, as_, ar,
                     [lanes(ahead, ahead), lanes(behind, behind), lanes(ahead, behind), own_live[:1]],
                 )
+                for copy in gcopy:
+                    copy.start()
             near = pright[pl.ds(c + cells, PROWS, stride=ext), :].astype(jnp.bfloat16)
             both = jnp.dot(
                 pturned[pl.ds(c * LANES, SPAN * LANES), :], near,

time: 58.9 us -> 57.7 us (0.980)
  Pallas kernels: 55.6 us -> 54.4 us
    pallas_call x1, Pallas kernels: 55.6 us -> 54.4 us  [body(): pl.pallas_call(functools.partial(kernel, n, ni, cells), out_shape=(jax.Sh...]
where the time goes in v5:
time: 57.7 us; the launch traced here: 57.5 us
  Pallas kernels  54.4 us (94%)
  local copies, waits for them, and re-layouts  1.82 us (3%)
  between operations  1.29 us (2%)
    pallas_call x1, Pallas kernels, body(): pl.pallas_call(functools.partial(kernel, n, ni, cells), out_shape=(jax.Sh...  54.4 us
    unnamed x4, local copies, waits for them, and re-layouts  1.82 us

profile of v5, /device:TPU:0, one launch (start us, length us, event | category | flops | bytes accessed | tf_op | source)
XLA Modules:
  0.0 57.5 jit_solution(887854075016865460)
XLA Ops:
  1.3 54.4 %shard_map.77 = (f32[3,8,128]{2,1,0:T(8,128)}, f32[1,3]{1,0:T(1,128)}) custom-call(f32[3,8,128]{2,1,0:T(8,128)} %bitcast.10, f32[3,16,128]{2,1,0:T(8,128)} %bitcast.8, s32[8,128]{1,0:T(8,128)} %bitcast.11, s32[8,5]{1,0:T(8,128)} %pcells.1, s32[8,5]{1,0:T(8,128)} %plive.1, f32[1]{0:T(128)S(6)} %copy.14.spring_ref), custom_call_target="tpu_custom_call" | custom-call | tf_op jit(solution)/shard_map/pallas_call | solution.py:315
  55.7 0.0 copy-start
  55.7 1.3 %copy.15 = f32[1,3,1024]{2,0,1:T(1,128)} copy(f32[1,3,1024]{2,0,1:T(1,128)} %bitcast.9) | data formatting | bytes 24576
  57.0 0.0 copy-done
  57.0 0.5 copy.16
Async XLA Ops:
  55.7 1.3 %copy-start = (f32[1,3]{1,0:T(1,128)S(1)}, f32[1,3]{1,0:T(1,128)}, u32[]{:S(2)}) copy-start(f32[1,3]{1,0:T(1,128)} %get-tuple-element.13) | copy-start | bytes 40
